TPU v7x, 512 devices: a whole 4x4x16 slice. The times are simulated.
512 devices in a mesh: tm: 64 (over y, z), rows: 8 (over x, core).
Axes of the slice: x: 4, y: 4, z: 16, core: 2. Of those that a mesh axis runs over, the one named last changes fastest.
Arguments:
- states: float32 [128, 64, 640], P('tm'), may hold values from -6 to 6
- ancestors: int32 [128, 640], P('tm'), may hold values from 0 to 639
- tracer_obs: float32 [128, 32], P('tm'), may hold values from -6 to 6
- jitter: float32 [128], P('tm'), may hold values from 0.00390625 to 0.0390625
- fingerprints: float32 [64, 32], replicated, may hold values from -0.75 to 0.75
- tracer_scale: float32 [32], replicated, may hold values from 0.15 to 0.45
- prior_weights: float32 [640], replicated, may hold values from 0.25 to 4
Outputs:
- filtered: float32 [128, 640], P('tm', 'rows')
All inputs are finite; a program needn't handle non-finite values.
Results may differ from a plain program's by a relative error of at most 0.0003.
Values sent between devices are 32-bit elements; how exact they have to be, the bound alone decides.
A program may use at most 64 MiB of HBM per device.

v0:
```python
import jax
import jax.numpy as jnp
from jax import lax
from jax.sharding import PartitionSpec as P


def shifted(block, axis, distance):
    devices = range(lax.axis_size(axis))
    route = [(i - distance, i) for i in devices if i - distance in devices]
    return lax.ppermute(block, axis, route)


def transition(previous, current, parent_ids, observed, mixing, fingerprints, tracer_scale):
    count = current.shape[1]
    highest = lax.Precision.HIGHEST
    inner_prod = lax.dot_general(
        previous,
        current,
        (((0,), (0,)), ((), ())),
        precision=highest,
        preferred_element_type=jnp.float32,
    )
    distance = (
        jnp.sum(previous * previous, axis=0)[:, None]
        + jnp.sum(current * current, axis=0)[None, :]
        - 2.0 * inner_prod
    )
    kernel = jnp.exp(-2.0 * distance / current.shape[0])
    predicted = lax.dot_general(
        fingerprints,
        current,
        (((0,), (0,)), ((), ())),
        precision=highest,
        preferred_element_type=jnp.float32,
    )
    misfit = tracer_scale[:, None] * (observed[:, None] - predicted)
    likelihood = jnp.exp(-0.5 * jnp.sum(misfit * misfit, axis=0))
    parent = (parent_ids[None, :] == jnp.arange(count, dtype=jnp.int32)[:, None]).astype(
        jnp.float32
    )
    weight = likelihood[None, :] * (parent + mixing * kernel)
    return weight * (count / jnp.sum(weight))


def shards(states, ancestors, tracer_obs, jitter, fingerprints, tracer_scale, prior_weights):
    highest = lax.Precision.HIGHEST
    count = states.shape[2]
    own_rows = count // lax.axis_size("rows")
    row_start = lax.axis_index("rows") * own_rows
    time_index = lax.axis_index("tm")
    rim = shifted(states[-1], "tm", 1)
    local_ids = row_start + lax.broadcasted_iota(jnp.int32, (own_rows, count), 0)
    column_ids = lax.broadcasted_iota(jnp.int32, (own_rows, count), 1)
    block_init = (local_ids == column_ids).astype(jnp.float32)

    def accumulate(carry, inputs):
        running, previous = carry
        current, parent_ids, observed, mixing = inputs
        matrix = transition(
            previous, current, parent_ids, observed, mixing, fingerprints, tracer_scale
        )
        running = jnp.dot(running, matrix, precision=highest, preferred_element_type=jnp.float32)
        kept = lax.dynamic_slice_in_dim(matrix, row_start, own_rows, 0)
        return ((running, current), kept)

    (block_part, unused), kept_rows = lax.scan(
        accumulate, (block_init, rim), (states, ancestors, tracer_obs, jitter)
    )
    full_block = lax.all_gather(block_part, "rows", axis=0, tiled=True)
    start = prior_weights / jnp.sum(prior_weights)

    def turn(turn_index, incoming):
        moved = jnp.dot(incoming, full_block, precision=highest, preferred_element_type=jnp.float32)
        moved = moved / jnp.sum(moved)
        received = shifted(moved, "tm", 1)
        return jnp.where(time_index == 0, start, received)

    incoming = lax.fori_loop(0, lax.axis_size("tm") - 1, turn, start)

    def propagate(weights_now, kept):
        mine = lax.dynamic_slice_in_dim(weights_now, row_start, own_rows, 0)
        partial_term = jnp.dot(mine, kept, precision=highest, preferred_element_type=jnp.float32)
        moved = lax.psum(partial_term, "rows")
        moved = moved / jnp.sum(moved)
        return (moved, count * lax.dynamic_slice_in_dim(moved, row_start, own_rows, 0))

    unused_last, filtered = lax.scan(propagate, incoming, kept_rows)
    return filtered


def solution(mesh):
    return jax.shard_map(
        shards,
        mesh=mesh,
        in_specs=(P("tm", None, None), P("tm", None), P("tm", None), P("tm"), P(), P(), P()),
        out_specs=P("tm", "rows"),
        check_vma=False,
    )
```

profile of v0, /device:TPU:25, one launch (start us, length us, event | category | flops | bytes accessed | tf_op | source)
XLA Modules:
  0.0 808.5 jit_solution(13679982750202817545)
XLA Ops:
  11.1 11.5 %collective-permute-done.1 = f32[64,640]{1,0:T(8,128)S(1)} collective-permute-done((f32[64,640]{1,0:T(8,128)S(1)}, f32[64,640]{1,0:T(8,128)S(1)}, u32[]{:S(2)}, u32[]{:S(2)}) %collective-permute-start.1) | collective-permute-done | bytes 163872 | tf_op jit(solution)/shard_map/ppermute | solution.py:10
  22.7 20.1 %while.42 = (s32[]{:T(128)}, f32[80,640]{1,0:T(8,128)S(1)}, f32[64,640]{1,0:T(8,128)S(1)}, f32[2,80,640]{2,1,0:T(8,128)S(1)}, f32[32]{0:T(128)}, /*index=5*/f32[...) while((s32[]{:T(128)}, f32[80,640]{1,0:T(8,128)S(1)}, ...), condition=%wide.region_6.7_spmd, body=%wide.region_1.6_spmd.sunk | while | flops 728267520 | bytes 9130165 | solution.py:66
  44.9 29.3 %all-gather.2.cloned.1.call-done = f32[640,640]{1,0:T(8,128)} async-done(((f32[80,640]{1,0:T(8,128)}), f32[640,640]{1,0:T(8,128)}) %all-gather.2.cloned.1.call-update) | async-done | bytes 1638416 | tf_op jit(solution)/shard_map/all_gather | solution.py:69
  74.2 626.8 %while.43 = (s32[]{:T(128)}, f32[640]{0:T(1024)S(1)}, pred[]{:T(512)}, f32[640,640]{1,0:T(8,128)}, f32[640]{0:T(1024)S(1)}, /*index=5*/s32[]{:T(128)}, f32[]{:T(128)}) while((s32[]{:T(128)}, f32[640]{0:T(1024)S(1)}, pred[]{:T(512)}, f32[640,640]{1,0:T(8,128)}, f32[640]{0:T(1024)S(1)}, /*index=5*/s32[]{:T(128)}, f32[]{:T(128)}) %tuple.76), condition=%wide.region_9.10_spmd, body=%wide.region_7.9_spmd.sunk | while | flops 4917121 | bytes 1674370 | solution.py:78
  90.0 4.5 collective-permute-done
  100.0 4.5 collective-permute-done
  109.9 4.5 collective-permute-done
  119.8 4.5 collective-permute-done
  129.8 4.5 collective-permute-done
  139.7 4.5 collective-permute-done
  149.7 4.5 collective-permute-done
  159.6 4.5 collective-permute-done
  169.5 4.5 collective-permute-done
  179.5 4.5 collective-permute-done
  189.4 4.5 collective-permute-done
  199.4 4.5 collective-permute-done
  209.3 4.5 collective-permute-done
  229.2 4.5 collective-permute-done
  259.0 4.5 collective-permute-done
  278.9 4.5 collective-permute-done
  288.8 4.5 collective-permute-done
  308.7 4.5 collective-permute-done
  318.7 4.5 collective-permute-done
  338.5 4.5 collective-permute-done
  358.4 4.5 collective-permute-done
  368.4 4.5 collective-permute-done
  388.2 4.5 collective-permute-done
  398.2 4.5 collective-permute-done
  418.1 4.5 collective-permute-done
  447.9 4.5 collective-permute-done
  457.8 4.6 collective-permute-done
  477.8 4.5 collective-permute-done
  497.6 4.5 collective-permute-done
  507.6 4.5 collective-permute-done
  527.5 4.5 collective-permute-done
  537.4 4.5 collective-permute-done
  557.3 4.5 collective-permute-done
  587.1 4.5 collective-permute-done
  607.0 4.5 collective-permute-done
  616.9 4.5 collective-permute-done
  636.8 4.5 collective-permute-done
  646.8 4.5 collective-permute-done
  666.6 4.5 collective-permute-done
  686.5 4.5 collective-permute-done
  696.5 4.5 collective-permute-done
  701.0 100.1 %while.44 = (s32[]{:T(128)}, f32[640]{0:T(1024)S(1)}, f32[2,80]{1,0:T(2,128)S(1)}, s32[]{:T(128)}, f32[2,80,640]{2,1,0:T(8,128)S(1)}, /*index=5*/s32[]{:T(128)}, f32[]{:T(128)}, s32[]{:T(128)}) while((s32[]{:T(128)}, f32[640]{0:T(1024)S(1)}, f32[2,80]{1,0:T(2,128)S(1)}, s32[]{:T(128)}, f32[2,80,640]{2,1,0:T(8,128)S(1)}, ...), condition=%wide.region_13.14_spmd, body=%wide.region_10.13_spmd.sunk | while | flops 616401 | bytes 222065 | solution.py:87
  701.3 84.1 %psum.10 = f32[640]{0:T(1024)S(1)} all-reduce(f32[640]{0:T(1024)S(1)} %convolution_reduce_fusion.5), channel_id=1, replica_groups=mesh['tm'=64,'rows'=8] {'rows'}, use_global_device_ids=true, to_apply=%region_11.11 | all-reduce | flops 640 | bytes 5120 | tf_op jit(solution)/shard_map/while/body/eval_jaxpr/psum | solution.py:83
  787.2 12.4 %psum.10 = f32[640]{0:T(1024)S(1)} all-reduce(f32[640]{0:T(1024)S(1)} %convolution_reduce_fusion.5), channel_id=1, replica_groups=mesh['tm'=64,'rows'=8] {'rows'}, use_global_device_ids=true, to_apply=%region_11.11 | all-reduce | flops 640 | bytes 5120 | tf_op jit(solution)/shard_map/while/body/eval_jaxpr/psum | solution.py:83
  (451 shorter events, 469.3 us)
Async XLA Ops:
  6.5 67.7 %all-gather.2.cloned.1.call-start = ((), (), s32[]{:S(2)}) async-start(), calls=%async_computation | async-start | bytes 1843200 | tf_op jit(solution)/shard_map/all_gather | solution.py:69
  7.5 15.2 %collective-permute-start.1 = (f32[64,640]{1,0:T(8,128)S(1)}, f32[64,640]{1,0:T(8,128)S(1)}, u32[]{:S(2)}, u32[]{:S(2)}) collective-permute-start(f32[64,640]{1,0:T(8,128)S(1)} %slice_bitcast_fusion), channel_id=1, source_target_pairs={{0,8},{8,16},{16,24},{24,32},{32,40},{40,48},{48,56},{56,64},{64,7... | collective-permute-start | bytes 491528 | tf_op jit(solution)/shard_map/ppermute | solution.py:10
  77.7 6.9 collective-permute-start
  88.1 6.5 collective-permute-start
  98.0 6.5 collective-permute-start
  108.0 6.5 collective-permute-start
  117.9 6.5 collective-permute-start
  127.8 6.5 collective-permute-start
  137.8 6.5 collective-permute-start
  147.7 6.5 collective-permute-start
  157.7 6.5 collective-permute-start
  167.6 6.5 collective-permute-start
  177.6 6.5 collective-permute-start
  187.5 6.5 collective-permute-start
  197.4 6.5 collective-permute-start
  207.4 6.5 collective-permute-start
  217.3 6.5 collective-permute-start
  227.3 6.5 collective-permute-start
  247.1 6.5 collective-permute-start
  257.1 6.5 collective-permute-start
  277.0 6.5 collective-permute-start
  286.9 6.5 collective-permute-start
  306.8 6.5 collective-permute-start
  316.7 6.5 collective-permute-start
  336.6 6.5 collective-permute-start
  356.5 6.5 collective-permute-start
  366.4 6.5 collective-permute-start
  386.3 6.5 collective-permute-start
  396.3 6.5 collective-permute-start
  416.1 6.5 collective-permute-start
  436.0 6.5 collective-permute-start
  446.0 6.5 collective-permute-start
  455.9 6.5 collective-permute-start
  475.8 6.5 collective-permute-start
  495.7 6.5 collective-permute-start
  505.7 6.5 collective-permute-start
  525.5 6.5 collective-permute-start
  535.5 6.5 collective-permute-start
  555.4 6.5 collective-permute-start
  575.2 6.5 collective-permute-start
  585.2 6.5 collective-permute-start
  605.1 6.5 collective-permute-start
  615.0 6.5 collective-permute-start
  634.9 6.5 collective-permute-start
  644.8 6.5 collective-permute-start
  664.7 6.5 collective-permute-start
  684.6 6.5 collective-permute-start
  694.5 6.5 collective-permute-start
  (20 other events, 131.9 us)
Sparse Core Ops, SparseCore 0:
  43.6 30.5 all-gather.1
where the time goes:
time: 813 us; the launch traced here: 809 us
  waiting for transfers between devices  326 us (40%)
  matrix products  159 us (20%)
  starting transfers between devices  126 us (15%)
  blocking collectives  96.5 us (12%)
  other arithmetic  77.8 us (10%)
  between operations  13.5 us (2%)
  local copies, waits for them, and re-layouts  8.18 us (1%)
    ppermute x64, waiting for transfers between devices, shifted(): return lax.ppermute(block, axis, route)  296 us
    dot_general x63, matrix products, turn(): jnp.dot(incoming, full_block, precision=highest, preferred_element_type=j...  147 us
    ppermute x64, starting transfers between devices, shifted(): return lax.ppermute(block, axis, route)  126 us
    psum x2, blocking collectives, propagate(): moved = lax.psum(partial_term, 'rows')  96.5 us
    reduce_sum x63, other arithmetic, turn(): moved = moved / jnp.sum(moved)  36.5 us
    div x63, other arithmetic, turn(): moved = moved / jnp.sum(moved)  34.5 us
    all_gather x1, waiting for transfers between devices, shards(): full_block = lax.all_gather(block_part, 'rows', axis=0, tiled=True)  29.3 us
  transfers between devices with their start and end apart: 65, of which 65 were waited for; matrix products, arithmetic and copies ran while one was open for 0% of the time, Pallas kernels for 0%

commit v1 on v0

--- a/solution.py
+++ b/solution.py
@@ -66,7 +66,12 @@
     (block_part, unused), kept_rows = lax.scan(
         accumulate, (block_init, rim), (states, ancestors, tracer_obs, jitter)
     )
-    full_block = lax.all_gather(block_part, "rows", axis=0, tiled=True)
+    ring = [block_part]
+    for hop in range(7):
+        ring.append(lax.ppermute(ring[-1], "rows", [(dev, (dev + 1) % 8) for dev in range(8)]))
+    full_block = jnp.roll(
+        jnp.concatenate(ring[::-1], axis=0), (lax.axis_index("rows") + 1) * ring[0].shape[0], axis=0
+    )
     start = prior_weights / jnp.sum(prior_weights)
 
     def turn(turn_index, incoming):

time: 813 us -> 735 us (0.904)
  matrix products: 159 us -> 68.3 us
  between operations: 13.5 us -> 0.23 us
  starting transfers between devices: 126 us -> 137 us
  other arithmetic: 77.8 us -> 88.5 us
    dot_general x63, matrix products: 147 us -> 56.9 us  [turn(): jnp.dot(incoming, full_block, precision=highest, preferred_element_type=j...]
    all_gather x1 -> x0, waiting for transfers between devices: 29.3 us -> none  [shards(): full_block = lax.all_gather(block_part, 'rows', axis=0, tiled=True)]
    ppermute x0 -> x7, waiting for transfers between devices: none -> 27.4 us  [shards(): lax.ppermute(ring[-1], 'rows', [(dev, (dev + 1) % 8) for dev in range(8)])]
    ppermute x0 -> x7, starting transfers between devices: none -> 12 us  [shards(): lax.ppermute(ring[-1], 'rows', [(dev, (dev + 1) % 8) for dev in range(8)])]
  transfers between devices with their start and end apart: 65 -> 71, of which waited for: 65 -> 71; matrix products, arithmetic and copies ran while one was open for 0% -> 0% of each run, Pallas kernels for 0% -> 0%
where the time goes in v1:
time: 735 us; the launch traced here: 731 us
  waiting for transfers between devices  325 us (44%)
  starting transfers between devices  137 us (19%)
  blocking collectives  102 us (14%)
  other arithmetic  88.5 us (12%)
  matrix products  68.3 us (9%)
  local copies, waits for them, and re-layouts  7.72 us (1%)
    ppermute x64, waiting for transfers between devices, shifted(): return lax.ppermute(block, axis, route)  298 us
    ppermute x64, starting transfers between devices, shifted(): return lax.ppermute(block, axis, route)  125 us
    psum x2, blocking collectives, propagate(): moved = lax.psum(partial_term, 'rows')  102 us
    dot_general x63, matrix products, turn(): jnp.dot(incoming, full_block, precision=highest, preferred_element_type=j...  56.9 us
    reduce_sum x63, other arithmetic, turn(): moved = moved / jnp.sum(moved)  42.5 us
    div x63, other arithmetic, turn(): moved = moved / jnp.sum(moved)  39.9 us
    ppermute x7, waiting for transfers between devices, shards(): lax.ppermute(ring[-1], 'rows', [(dev, (dev + 1) % 8) for dev in range(8)])  27.4 us
  transfers between devices with their start and end apart: 71, of which 71 were waited for; matrix products, arithmetic and copies ran while one was open for 0% of the time, Pallas kernels for 0%

profile of v1, /device:TPU:25, one launch (start us, length us, event | category | flops | bytes accessed | tf_op | source)
XLA Modules:
  0.0 730.6 jit_solution(13071629017219384681)
XLA Ops:
  4.6 11.5 %collective-permute-done.1 = f32[64,640]{1,0:T(8,128)S(1)} collective-permute-done((f32[64,640]{1,0:T(8,128)S(1)}, f32[64,640]{1,0:T(8,128)S(1)}, u32[]{:S(2)}, u32[]{:S(2)}) %collective-permute-start.1) | collective-permute-done | bytes 163872 | tf_op jit(solution)/shard_map/ppermute | solution.py:10
  16.2 19.9 %while.42 = (s32[]{:T(128)}, f32[80,640]{1,0:T(8,128)S(1)}, f32[64,640]{1,0:T(8,128)S(1)}, f32[2,80,640]{2,1,0:T(8,128)S(1)}, f32[32]{0:T(128)}, /*index=5*/f32[...) while((s32[]{:T(128)}, f32[80,640]{1,0:T(8,128)S(1)}, ...), condition=%wide.region_6.7_spmd, body=%wide.region_1.6_spmd.sunk | while | flops 728267520 | bytes 9130165 | solution.py:66
  59.1 4.7 collective-permute-done.6
  64.9 5.3 collective-permute-done.7
  70.8 5.8 collective-permute-done.8
  77.1 548.2 %while.43 = (s32[]{:T(128)}, f32[640]{0:T(1024)S(1)}, pred[]{:T(512)}, f32[640,640]{1,0:T(8,128)S(1)}, f32[640]{0:T(1024)S(1)}, /*index=5*/s32[]{:T(128)}, f32[]{:T(128)}) while((s32[]{:T(128)}, f32[640]{0:T(1024)S(1)}, pred[]{:T(512)}, f32[640,640]{1,0:T(8,128)S(1)}, f32[640]{0:T(1024)S(1)}, /*index=5*/s32[]{:T(128)}, f32[]{:T(128)}) %tuple.76), condition=%wide.region_9.10_spmd, body=%wide.region_7.9_spmd.sunk | while | flops 4917121 | bytes 1674370 | solution.py:83
  81.3 4.5 collective-permute-done
  90.0 4.5 collective-permute-done
  98.7 4.5 collective-permute-done
  107.4 4.5 collective-permute-done
  116.1 4.5 collective-permute-done
  124.8 4.5 collective-permute-done
  142.2 4.5 collective-permute-done
  159.5 4.5 collective-permute-done
  168.2 4.5 collective-permute-done
  185.6 4.9 collective-permute-done
  194.6 4.5 collective-permute-done
  212.0 4.5 collective-permute-done
  229.4 4.5 collective-permute-done
  238.1 4.5 collective-permute-done
  255.5 4.5 collective-permute-done
  272.9 4.5 collective-permute-done
  290.3 4.5 collective-permute-done
  298.9 4.5 collective-permute-done
  316.3 4.5 collective-permute-done
  333.7 4.5 collective-permute-done
  351.1 4.5 collective-permute-done
  359.8 4.5 collective-permute-done
  377.2 4.5 collective-permute-done
  394.6 4.5 collective-permute-done
  403.3 4.5 collective-permute-done
  420.6 4.5 collective-permute-done
  438.0 4.5 collective-permute-done
  455.4 4.5 collective-permute-done
  464.1 4.5 collective-permute-done
  481.5 4.5 collective-permute-done
  498.9 4.5 collective-permute-done
  516.3 4.5 collective-permute-done
  525.0 4.5 collective-permute-done
  542.3 4.5 collective-permute-done
  559.7 4.8 collective-permute-done
  568.7 4.5 collective-permute-done
  586.1 4.5 collective-permute-done
  594.8 4.5 collective-permute-done
  612.1 4.5 collective-permute-done
  625.4 104.7 %while.44 = (s32[]{:T(128)}, f32[640]{0:T(1024)S(1)}, f32[2,80]{1,0:T(2,128)S(1)}, s32[]{:T(128)}, f32[2,80,640]{2,1,0:T(8,128)S(1)}, /*index=5*/s32[]{:T(128)}, f32[]{:T(128)}, s32[]{:T(128)}) while((s32[]{:T(128)}, f32[640]{0:T(1024)S(1)}, f32[2,80]{1,0:T(2,128)S(1)}, s32[]{:T(128)}, f32[2,80,640]{2,1,0:T(8,128)S(1)}, ...), condition=%wide.region_13.14_spmd, body=%wide.region_10.13_spmd.sunk | while | flops 616401 | bytes 222065 | solution.py:92
  625.7 89.1 %psum.10 = f32[640]{0:T(1024)S(1)} all-reduce(f32[640]{0:T(1024)S(1)} %convolution_reduce_fusion.5), channel_id=1, replica_groups=mesh['tm'=64,'rows'=8] {'rows'}, use_global_device_ids=true, to_apply=%region_11.11 | all-reduce | flops 640 | bytes 5120 | tf_op jit(solution)/shard_map/while/body/eval_jaxpr/psum | solution.py:88
  716.4 12.4 %psum.10 = f32[640]{0:T(1024)S(1)} all-reduce(f32[640]{0:T(1024)S(1)} %convolution_reduce_fusion.5), channel_id=1, replica_groups=mesh['tm'=64,'rows'=8] {'rows'}, use_global_device_ids=true, to_apply=%region_11.11 | all-reduce | flops 640 | bytes 5120 | tf_op jit(solution)/shard_map/while/body/eval_jaxpr/psum | solution.py:88
  (477 shorter events, 421.5 us)
Async XLA Ops:
  0.9 15.2 %collective-permute-start.1 = (f32[64,640]{1,0:T(8,128)S(1)}, f32[64,640]{1,0:T(8,128)S(1)}, u32[]{:S(2)}, u32[]{:S(2)}) collective-permute-start(f32[64,640]{1,0:T(8,128)S(1)} %slice_bitcast_fusion), channel_id=1, source_target_pairs={{0,8},{8,16},{16,24},{24,32},{32,40},{40,48},{48,56},{56,64},{64,7... | collective-permute-start | bytes 491528 | tf_op jit(solution)/shard_map/ppermute | solution.py:10
  79.4 6.5 collective-permute-start
  88.1 6.5 collective-permute-start
  96.8 6.5 collective-permute-start
  105.5 6.5 collective-permute-start
  114.1 6.5 collective-permute-start
  122.8 6.5 collective-permute-start
  131.5 6.5 collective-permute-start
  140.2 6.5 collective-permute-start
  148.9 6.5 collective-permute-start
  157.6 6.5 collective-permute-start
  166.3 6.5 collective-permute-start
  175.0 6.5 collective-permute-start
  183.7 6.8 collective-permute-start
  192.7 6.5 collective-permute-start
  201.4 6.5 collective-permute-start
  210.1 6.5 collective-permute-start
  218.8 6.5 collective-permute-start
  227.5 6.5 collective-permute-start
  236.2 6.5 collective-permute-start
  244.9 6.5 collective-permute-start
  253.6 6.5 collective-permute-start
  270.9 6.5 collective-permute-start
  288.3 6.5 collective-permute-start
  297.0 6.5 collective-permute-start
  314.4 6.5 collective-permute-start
  331.8 6.5 collective-permute-start
  349.2 6.5 collective-permute-start
  357.9 6.5 collective-permute-start
  375.3 6.5 collective-permute-start
  392.6 6.5 collective-permute-start
  401.3 6.5 collective-permute-start
  410.0 6.5 collective-permute-start
  418.7 6.5 collective-permute-start
  436.1 6.5 collective-permute-start
  453.5 6.5 collective-permute-start
  462.2 6.5 collective-permute-start
  479.6 6.5 collective-permute-start
  496.9 6.5 collective-permute-start
  514.3 6.5 collective-permute-start
  523.0 6.5 collective-permute-start
  540.4 6.5 collective-permute-start
  557.8 6.7 collective-permute-start
  566.8 6.5 collective-permute-start
  584.1 6.5 collective-permute-start
  592.8 6.5 collective-permute-start
  601.5 6.5 collective-permute-start
  610.2 6.5 collective-permute-start
  (25 other events, 192.6 us)
